TPU v7x, 768 devices: a whole 4x8x12 slice. The times are simulated.
768 devices in a mesh: dp: 16 (over z_lo, x), fsdp: 48 (over y, z_hi, core).
Axes of the slice: x: 4, y: 8, z: 12 (z_hi: 3, z_lo: 4; z = z_hi * 4 + z_lo), core: 2. Of those that a mesh axis runs over, the one named last changes fastest.
Arguments:
- hidden: bfloat16 [768, 256, 5120], P(('dp', 'fsdp')), may hold values from -6 to 6
- queries: bfloat16 [768, 256, 1024], P(('dp', 'fsdp')), may hold values from -6 to 6
- upstream: bfloat16 [768, 256, 1024], P(('dp', 'fsdp')), may hold values from -0.3984375 to 0.3984375
- advantage: float32 [768, 256], P(('dp', 'fsdp')), may hold values from -5 to 5
- selected: int32 [768, 256], P(('dp', 'fsdp')), may hold values from 0 to 1, as said below
- segment: int32 [768, 256], P(('dp', 'fsdp')), may hold values from 0 to 3, never falling along the last dimension, each value on 1 to 128 neighbouring positions
- w_kv: bfloat16 [5376, 256], P('fsdp'), may hold values from -0.078125 to 0.078125
- k_gain: float32 [128], replicated, may hold values from 0.25 to 1.75
- q_gain: float32 [128], replicated, may hold values from 0.25 to 1.75
Outputs:
- d_weight: float32 [5376, 256], P('fsdp')
- d_gain: float32 [128], replicated
Inputs may be any that keep to these rules, and one draw needn't show every extreme that they name: Each row has at most 128 selected tokens, and some row has exactly 128.
All inputs are finite; a program needn't handle non-finite values.
Results may differ from a plain program's by a relative error of at most 0.007.
Values may be sent and summed in bfloat16 or wider, within the bound.
No kernel may reach another device: no remote copies, remote signals or barrier semaphores. Data moves between devices by JAX's collectives and lax.ppermute only.
A program may use at most 32 MiB of HBM per device.

v0:
```python
import jax
import jax.numpy as jnp
from jax import lax
from jax.sharding import PartitionSpec as P

epsilon = 1e-06


def attend(q_rows, g_rows, q_place, q_group, k_norm, values, k_place, k_group, score_scale):
    allowed = (q_group[:, None] == k_group[None, :]) & (k_place[None, :] <= q_place[:, None])
    scores = (
        jnp.einsum("qhd,kd->hqk", q_rows, k_norm, preferred_element_type=jnp.float32) * score_scale
    )
    expo = jnp.where(allowed[None], jnp.exp(scores), 0.0)
    probs = expo / jnp.sum(expo, axis=-1, keepdims=True)
    probs_b = probs.astype(jnp.bfloat16)
    outputs = jnp.einsum("hqk,kd->qhd", probs_b, values, preferred_element_type=jnp.float32)
    delta = jnp.sum(g_rows.astype(jnp.float32) * outputs, axis=-1)
    dprob = jnp.einsum("qhd,kd->hqk", g_rows, values, preferred_element_type=jnp.float32)
    dscore = (probs * (dprob - delta.T[:, :, None]) * score_scale).astype(jnp.bfloat16)
    d_key = jnp.einsum("hqk,qhd->kd", dscore, q_rows, preferred_element_type=jnp.float32)
    d_value = jnp.einsum("hqk,qhd->kd", probs_b, g_rows, preferred_element_type=jnp.float32)
    return (d_key, d_value)


def shards(hidden, queries, upstream, advantage, selected, segment, w_kv, k_gain, q_gain):
    hidden_row = hidden[0]
    length = hidden_row.shape[0]
    width = hidden_row.shape[1]
    rows_dev = w_kv.shape[0]
    head_dim = k_gain.shape[0]
    heads = queries.shape[2] // head_dim
    owners = lax.axis_size("fsdp")
    padded_width = rows_dev * owners
    hidden_pad = jnp.pad(hidden_row, ((0, 0), (0, padded_width - width)))
    columns = hidden_pad
    key_value = jnp.dot(
        columns,
        lax.all_gather(w_kv, "fsdp", axis=0, tiled=True),
        preferred_element_type=jnp.float32,
    )
    k_raw = key_value[:, :head_dim]
    k_scale = lax.rsqrt(jnp.mean(k_raw * k_raw, axis=-1, keepdims=True) + epsilon)
    k_hat = k_raw * k_scale
    k_norm = (k_hat * k_gain).astype(jnp.bfloat16)
    values = key_value[:, head_dim:].astype(jnp.bfloat16)
    query_full = queries[0].reshape(length, heads, head_dim).astype(jnp.float32)
    q_scale = lax.rsqrt(jnp.mean(query_full * query_full, axis=-1, keepdims=True) + epsilon)
    q_norm = (query_full * q_scale * q_gain).astype(jnp.bfloat16)
    token_weight = advantage[0] * selected[0].astype(jnp.float32)
    cotangent = (token_weight[:, None] * upstream[0].astype(jnp.float32)).astype(jnp.bfloat16)
    cotangent = cotangent.reshape(length, heads, head_dim)
    positions = jnp.arange(length, dtype=jnp.int32)
    segment_row = segment[0]
    score_scale = head_dim ** (-0.5)
    d_key, d_value = attend(
        q_norm,
        cotangent,
        positions,
        segment_row,
        k_norm,
        values,
        positions,
        segment_row,
        score_scale,
    )
    d_khat = d_key * k_gain
    gain_term = jnp.sum(d_key * k_hat, axis=0)
    d_kraw = k_scale * (d_khat - k_hat * jnp.mean(d_khat * k_hat, axis=-1, keepdims=True))
    d_kv = jnp.concatenate([d_kraw, d_value], axis=1).astype(jnp.bfloat16)
    columns = hidden_pad
    owned = lax.psum_scatter(
        lax.dot_general(
            columns, d_kv, (((0,), (0,)), ((), ())), preferred_element_type=jnp.float32
        ),
        "fsdp",
        scatter_dimension=0,
        tiled=True,
    )
    d_weight = lax.psum(owned, "dp")
    d_gain = lax.psum(gain_term, ("dp", "fsdp"))
    return (d_weight, d_gain)


def solution(mesh):
    in_specs = (
        P(("dp", "fsdp"), None, None),
        P(("dp", "fsdp"), None, None),
        P(("dp", "fsdp"), None, None),
        P(("dp", "fsdp"), None),
        P(("dp", "fsdp"), None),
        P(("dp", "fsdp"), None),
        P("fsdp", None),
        P(),
        P(),
    )
    out_specs = (P("fsdp", None), P())
    return jax.shard_map(shards, mesh=mesh, in_specs=in_specs, out_specs=out_specs, check_vma=False)
```

profile of v0, /device:TPU:1, one launch (start us, length us, event | category | flops | bytes accessed | tf_op | source)
XLA Modules:
  0.0 534.5 jit_solution(12014076031823255166)
XLA Ops:
  7.2 0.0 all-gather.2.cloned.1.call-start
  7.2 0.7 all-gather.2.cloned.1.call-update
  7.9 0.0 reduce-scatter.2.cloned.1.call-start
  7.9 1.1 convert_bitcast_fusion.1
  9.1 0.0 copy-start.9
  9.1 0.2 copy.41
  9.3 0.0 copy-start.2
  9.3 0.3 multiply_reduce_fusion
  9.7 0.1 copy.20
  9.7 0.1 copy.21
  9.9 0.0 copy-done.9
  9.9 0.3 multiply_convert_fusion
  10.2 0.0 copy-start.7
  10.3 0.0 copy-start.8
  10.3 1.1 copy.30
  11.4 0.0 copy-done.2
  11.4 0.1 convert_bitcast_fusion
  11.5 0.0 copy-start.6
  11.5 0.0 copy-start
  11.5 0.2 copy.42
  11.7 0.0 copy-done.7
  11.8 0.0 copy-done.8
  11.8 0.3 fusion.14
  12.1 1.1 copy.32
  13.3 0.0 copy-done.6
  13.3 0.1 fusion.19
  13.4 0.0 copy-start.5
  13.4 113.0 %all-gather.2.cloned.1.call-done = bf16[5376,256]{1,0:T(8,128)(2,1)} async-done(((bf16[112,256]{1,0:T(8,128)(2,1)}), bf16[5376,256]{1,0:T(8,128)(2,1)}) %all-gather.2.cloned.1.call-update) | async-done | bytes 2752528 | tf_op jit(solution)/shard_map/all_gather | solution.py:39
  126.4 0.0 copy-done
  126.4 0.0 copy-start.3
  126.4 0.0 copy-start.10
  126.4 3.0 fusion.2
  129.5 0.0 copy-done.3
  129.5 0.0 copy-done.10
  129.5 0.7 fusion.8
  130.2 0.0 copy-start.1
  130.2 0.0 copy-done.5
  130.2 1.3 copy-done.1
  131.6 1.4 fusion.18
  133.0 2.7 copy.27
  135.6 2.5 fusion.13
  138.1 1.7 fusion.11
  139.9 0.1 copy.28
  139.9 0.0 copy-start.4
  139.9 3.0 multiply_reduce_fusion.1
  142.9 0.1 multiply_convert_fusion.1
  143.0 0.0 copy-done.4
  143.0 3.3 fusion
  146.4 0.0 reduce-scatter.2.cloned.1.call-update
  146.4 0.0 all-reduce.3.cloned.1.call-start
  146.4 221.4 %reduce-scatter.2.cloned.1.call-done = f32[112,256]{1,0:T(8,128)} async-done(((f32[5376,256]{1,0:T(8,128)}), f32[112,256]{1,0:T(8,128)}) %reduce-scatter.2.cloned.1.call-update) | async-done | bytes 114704 | tf_op jit(solution)/shard_map/reduce_scatter | solution.py:72
  367.8 0.0 all-reduce.3.cloned.1.call-update
  367.8 110.1 %psum.15 = f32[128]{0:T(128)} all-reduce(f32[128]{0:T(128)S(1)} %get-tuple-element.2), channel_id=1, replica_groups=mesh['dp'=16,'fsdp'=48] {'dp','fsdp'}, use_global_device_ids=true, to_apply=%region_8.9 | all-reduce | flops 128 | bytes 1024 | tf_op jit(solution)/shard_map/psum | solution.py:81
  478.0 48.4 %all-reduce.3.cloned.1.call-done = f32[112,256]{1,0:T(8,128)} async-done(((f32[112,256]{1,0:T(8,128)}), f32[112,256]{1,0:T(8,128)}) %all-reduce.3.cloned.1.call-update) | async-done | bytes 114704 | tf_op jit(solution)/shard_map/psum | solution.py:80
  526.4 1.6 copy.44
  (5 shorter events, 0.1 us)
Async XLA Ops:
  7.2 119.2 %all-gather.2.cloned.1.call-start = ((), (), s32[]{:S(2)}) async-start(), calls=%async_computation.1 | async-start | bytes 2809856 | tf_op jit(solution)/shard_map/all_gather | solution.py:39
  7.9 359.9 %reduce-scatter.2.cloned.1.call-start = ((), (), s32[]{:S(2)}) async-start(), calls=%async_computation.2 | async-start | bytes 5619712 | tf_op jit(solution)/shard_map/reduce_scatter | solution.py:72
  9.1 0.8 copy-start.9
  9.3 2.1 copy-start.2
  10.2 1.5 copy-start.7
  10.3 1.5 copy-start.8
  11.5 1.8 copy-start.6
  11.5 114.9 %copy-start = (bf16[1,256,5120]{2,1,0:T(8,128)(2,1)S(1)}, bf16[1,256,5120]{2,1,0:T(8,128)(2,1)}, u32[]{:S(2)}) copy-start(bf16[1,256,5120]{2,1,0:T(8,128)(2,1)} %param.9) | copy-start | bytes 7864324
  13.4 116.9 %copy-start.5 = (pred[256,256]{0,1:T(8,128)(4,1)}, pred[256,256]{0,1:T(8,128)(4,1)S(1)}, u32[]{:S(2)}) copy-start(pred[256,256]{0,1:T(8,128)(4,1)S(1)} %fusion.19) | copy-start | bytes 196612
  126.4 3.1 copy-start.3
  126.4 3.1 copy-start.10
  130.2 1.4 copy-start.1
  139.9 3.1 copy-start.4
  146.4 380.0 %all-reduce.3.cloned.1.call-start = ((), (), s32[]{:S(2)}) async-start(), calls=%async_computation.3 | async-start | bytes 229376 | tf_op jit(solution)/shard_map/psum | solution.py:80
Sparse Core Ops, SparseCore 0:
  12.0 114.3 all-gather.1
  146.5 221.2 reduce-scatter.1
  371.0 155.3 all-reduce.2
where the time goes:
time: 545 us; the launch traced here: 534 us
  waiting for transfers between devices  384 us (70%)
  blocking collectives  110 us (20%)
  matrix products  14.3 us (3%)
  between operations  14 us (3%)
  local copies, waits for them, and re-layouts  8.52 us (2%)
    reduce_scatter x1, waiting for transfers between devices, shards(): lax.psum_scatter(lax.dot_general(columns, d_kv, (((0,), (0,)), ((), ())),...  221 us
    all_gather x1, waiting for transfers between devices, shards(): lax.all_gather(w_kv, 'fsdp', axis=0, tiled=True)  113 us
    psum x1, blocking collectives, shards(): d_gain = lax.psum(gain_term, ('dp', 'fsdp'))  110 us
    psum x1, waiting for transfers between devices, shards(): d_weight = lax.psum(owned, 'dp')  48.4 us
  transfers between devices with their start and end apart: 3, of which 3 were waited for; matrix products, arithmetic and copies ran while one was open for 1% of the time, Pallas kernels for 0%

commit v1 on v0

v1 whole, which is shorter than its diff:
```python
import jax
import jax.numpy as jnp
from jax import lax
from jax.experimental import pallas as pl
from jax.experimental.pallas import tpu as pltpu
from jax.sharding import Mesh, PartitionSpec as P

EPS = 1e-06
HD = 128
GROUP = 8
TOK = 256
D = 5120
OWN = 112
HALF = OWN // 2
NEAR = 8
FAR = 12
BODY = FAR * HALF
SPAN = 48 * OWN
AXES = ("zh", "zl", "xh", "xl", "yh", "yl", "zhi", "core")
PAIRS = ("zl", "xl", "yl")

f32 = jnp.float32
bf16 = jnp.bfloat16
vmem = pl.BlockSpec(memory_space=pltpu.VMEM)
smem = pl.BlockSpec(memory_space=pltpu.SMEM)


def dot(a, b, ca, cb):
    return lax.dot_general(a, b, (((ca,), (cb,)), ((), ())), preferred_element_type=f32)


def column(row):
    return jnp.transpose(jnp.broadcast_to(row, (HD, TOK)))


def first_row(far, yl):
    return ((far // 3) * 6 + yl * 3 + far % 3) * (2 * OWN)


def place(w, ref, parity):
    def step(far, _):
        for yl in range(2):
            base = first_row(far, yl)
            row = pl.multiple_of(base + parity * OWN, 16)
            for ch in range(2):
                both = jnp.concatenate([ref[4 * ch + yl, far].astype(f32), ref[4 * ch + 2 + yl, far].astype(f32)], axis=0)
                w[pl.ds(row, OWN), ch * HD : (ch + 1) * HD] = both.astype(bf16)
            gap = pl.multiple_of(base + (1 - parity) * OWN, 16)
            w[pl.ds(gap, OWN), :] = jnp.zeros((OWN, 2 * HD), bf16)
        return 0

    lax.fori_loop(0, FAR, step, 0)


def prepare_body(where_ref, hidden, queries, upstream, advantage, selected, q_gain, own, q_out, cot_out, kv_out, w):
    place(w, own, where_ref[0])
    kv_out[...] = dot(hidden[...], w[:D, :], 1, 0)
    weight = column(advantage[...] * selected[...].astype(f32))
    for h in range(GROUP):
        cols = slice(h * HD, (h + 1) * HD)
        query = queries[:, cols].astype(f32)
        q_scale = lax.rsqrt(jnp.mean(query * query, axis=-1, keepdims=True) + EPS)
        q_out[:, cols] = (query * q_scale * q_gain[...]).astype(bf16)
        cot_out[:, cols] = (weight * upstream[:, cols].astype(f32)).astype(bf16)


def backward_body(where_ref, hidden, q_norms, cots, kv_part, segment, k_gain, other, keep, send, w, acc):
    core = where_ref[0]
    place(w, other, 1 - core)
    kv = kv_part[...] + dot(hidden[...], w[:D, :], 1, 0)
    k_raw = kv[:, :HD]
    k_scale = lax.rsqrt(jnp.mean(k_raw * k_raw, axis=-1, keepdims=True) + EPS)
    k_hat = k_raw * k_scale
    k_norm = (k_hat * k_gain[...]).astype(bf16)
    values = kv[:, HD:].astype(bf16)
    seg = segment[...].astype(f32)
    seg_col = column(seg)
    s_col = lax.broadcasted_iota(jnp.int32, (TOK, HD), 0)
    t_row = lax.broadcasted_iota(jnp.int32, (TOK, HD), 1)
    allowed = jnp.concatenate(
        [(seg_col == seg[:, i * HD : (i + 1) * HD]) & (s_col <= t_row + i * HD) for i in range(2)], axis=1
    )
    scale = HD ** (-0.5)
    d_key = jnp.zeros((TOK, HD), f32)
    d_value = jnp.zeros((TOK, HD), f32)
    for h in range(GROUP):
        cols = slice(h * HD, (h + 1) * HD)
        q_norm = q_norms[:, cols]
        cot = cots[:, cols]
        expo = jnp.where(allowed, jnp.exp(dot(k_norm, q_norm, 1, 1) * scale), 0.0)
        probs = expo * (1.0 / jnp.sum(expo, axis=0, keepdims=True))
        probs_b = probs.astype(bf16)
        dprob = dot(values, cot, 1, 1)
        delta = jnp.sum(probs_b.astype(f32) * dprob, axis=0, keepdims=True)
        dscore = (probs * (dprob - delta) * scale).astype(bf16)
        d_key = d_key + dot(dscore, q_norm, 1, 0)
        d_value = d_value + dot(probs_b, cot, 1, 0)
    gain = jnp.sum(d_key * k_hat, axis=0, keepdims=True)
    d_khat = d_key * k_gain[...]
    d_kraw = k_scale * (d_khat - k_hat * jnp.mean(d_khat * k_hat, axis=-1, keepdims=True))
    d_kv = jnp.concatenate([d_kraw, d_value], axis=1).astype(bf16)
    chunk = 1024
    for j in range(D // chunk):
        acc[j * chunk : (j + 1) * chunk, :] = dot(hidden[:, j * chunk : (j + 1) * chunk], d_kv, 0, 0)
    acc[D:SPAN, :] = jnp.zeros((SPAN - D, 2 * HD), f32)

    def put(far, _):
        for yl in range(2):
            base = first_row(far, yl)
            for parity, ref in ((core, keep), (1 - core, send)):
                for q in range(4):
                    row = pl.multiple_of(base + parity * OWN + (q % 2) * HALF, 8)
                    ref[2 * q + yl, far] = acc[pl.ds(row, HALF), (q // 2) * HD : (q // 2 + 1) * HD].astype(bf16)
        return 0

    lax.fori_loop(0, FAR, put, 0)
    high = gain.astype(bf16).astype(f32)
    line = lax.broadcasted_iota(jnp.int32, (HALF, HD), 0)
    rows = jnp.where(line == 0, high, jnp.where(line == 1, gain - high, 0.0)).astype(bf16)
    keep[1, FAR - 1] = rows
    send[1, FAR - 1] = rows


def gain_rows(pair):
    total = pair[0:1] + pair[1:2]
    high = total.astype(bf16).astype(f32)
    line = lax.broadcasted_iota(jnp.int32, (8, HD), 0)
    return jnp.where(line == 0, high, jnp.where(line == 1, total - high, 0.0))


def near_body(keep, received, blocks):
    tail = gain_rows(keep[1, FAR - 1, 0:8].astype(f32) + received[1, FAR - 1, 0:8].astype(f32))
    for i in range(NEAR):
        total = (keep[i].astype(f32) + received[i].astype(f32)).reshape(BODY, HD)
        blocks[i] = jnp.concatenate([total, tail], axis=0).astype(bf16)


def far_body(where_ref, received, blocks):
    tail = gain_rows(sum(received[i, BODY : BODY + 8].astype(f32) for i in range(NEAR)))
    for far in range(FAR):
        total = sum(received[i, far * HALF : (far + 1) * HALF].astype(f32) for i in range(NEAR))
        if far == FAR - 1:
            total = jnp.where(where_ref[1] == 1, 0.0, total)
        blocks[far] = jnp.concatenate([total, tail], axis=0).astype(bf16)


def last_body(received, blocks):
    total = sum(received[i].astype(f32) for i in range(FAR))
    whole = jnp.concatenate([total[:HALF], gain_rows(total[HALF:])], axis=0).astype(bf16)
    for i in range(16):
        blocks[i] = whole


def finish_body(spread, d_weight, d_gain):
    total = [sum(spread[8 * (i // 2) + 4 * (q // 2) + 2 * (i % 2) + q % 2].astype(f32) for i in range(4)) for q in range(4)]
    for q in range(4):
        row, col = (q % 2) * HALF, (q // 2) * HD
        d_weight[row : row + HALF, col : col + HD] = total[q][:HALF]
    d_gain[...] = total[0][HALF : HALF + 1] + total[0][HALF + 1 : HALF + 2]


def call(body, out, n_vector, scratch, limit, name, scalars=0):
    return pl.pallas_call(
        body,
        out_shape=out,
        in_specs=[smem] * scalars + [vmem] * n_vector,
        out_specs=jax.tree.map(lambda _: vmem, out),
        scratch_shapes=scratch,
        compiler_params=pltpu.CompilerParams(vmem_limit_bytes=limit << 20),
        name=name,
    )


def shape(*dims, dtype=bf16):
    return jax.ShapeDtypeStruct(dims, dtype)


def exchange(x, axes):
    return lax.all_to_all(x, axes, 0, 0, tiled=True)


def swap(x):
    return lax.ppermute(x, "core", [(0, 1), (1, 0)])


def shards(hidden, queries, upstream, advantage, selected, segment, w_kv, k_gain, q_gain):
    where = jnp.stack([lax.axis_index("core"), lax.axis_index("yl")]).astype(jnp.int32)
    mine = lax.dynamic_slice(w_kv, (lax.axis_index("xl") * HALF, lax.axis_index("zl") * HD), (HALF, HD))
    part = exchange(jnp.broadcast_to(mine[None], (FAR, HALF, HD)), ("yh", "zhi"))
    own = exchange(jnp.broadcast_to(part[None], (NEAR, FAR, HALF, HD)), PAIRS)
    other = swap(own)
    w_scratch = pltpu.VMEM((SPAN, 2 * HD), bf16)
    q_norms, cots, kv_part = call(
        prepare_body, (shape(TOK, GROUP * HD), shape(TOK, GROUP * HD), shape(TOK, 2 * HD, dtype=f32)), 7, [w_scratch], 16, "prepare", 1
    )(where, hidden[0], queries[0], upstream[0], advantage, selected, q_gain[None], own)
    piece = shape(NEAR, FAR, HALF, HD)
    keep, send = call(backward_body, (piece, piece), 7, [w_scratch, pltpu.VMEM((SPAN, 2 * HD), f32)], 24, "backward", 1)(
        where, hidden[0], q_norms, cots, kv_part, segment, k_gain[None], other
    )
    blocks = call(near_body, shape(NEAR, BODY + 8, HD), 2, [], 12, "near")(keep, swap(send))
    blocks = call(far_body, shape(FAR, HALF + 8, HD), 1, [], 12, "far", 1)(where, exchange(blocks, PAIRS))
    blocks = call(last_body, shape(16, HALF + 8, HD), 1, [], 8, "last")(exchange(blocks, ("yh", "zhi")))
    spread = exchange(blocks, ("zh", "zl", "xh", "xl"))
    d_weight, d_gain = call(finish_body, (shape(OWN, 2 * HD, dtype=f32), shape(1, HD, dtype=f32)), 1, [], 4, "finish")(spread)
    return (d_weight, d_gain[0])


def solution(mesh):
    fine = Mesh(mesh.devices.reshape(2, 2, 2, 2, 4, 2, 3, 2), AXES)
    rows = P(AXES, None, None)
    flat = P(AXES, None)
    owners = P(("yh", "yl", "zhi", "core"), None)
    in_specs = (rows, rows, rows, flat, flat, flat, owners, P(), P())
    return jax.shard_map(shards, mesh=fine, in_specs=in_specs, out_specs=(owners, P()), check_vma=False)
```

time: 545 us -> 136 us (0.25); the launches traced: 534 us -> 134 us
  waiting for transfers between devices: 384 us -> 3.1 us
  matrix products: 14.3 us -> 0 us
  between operations: 14 us -> 0.78 us
  Pallas kernels: 0 us -> 12.4 us
  starting transfers between devices: 0.12 us -> 7.43 us
  local copies, waits for them, and re-layouts: 8.52 us -> 2 us
    reduce_scatter x1 -> x0, waiting for transfers between devices: 221 us -> none  [shards(): lax.psum_scatter(lax.dot_general(columns, d_kv, (((0,), (0,)), ((), ())),...]
    all_gather x1 -> x0, waiting for transfers between devices: 113 us -> none  [shards(): lax.all_gather(w_kv, 'fsdp', axis=0, tiled=True)]
    psum x1 -> x0, blocking collectives: 110 us -> none  [shards(): d_gain = lax.psum(gain_term, ('dp', 'fsdp'))]
    all_to_all x0 -> x5, blocking collectives: none -> 109 us  [exchange(): return lax.all_to_all(x, axes, 0, 0, tiled=True)]
    psum x1 -> x0, waiting for transfers between devices: 48.4 us -> none  [shards(): d_weight = lax.psum(owned, 'dp')]
    dot_general x6 -> x0, matrix products: 14.3 us -> none  [the longest x1 3.32 us: shards(): lax.dot_general(columns, d_kv, (((0,), (0,)), ((), ())), preferred_elemen...]
    pallas_call x0 -> x6, Pallas kernels: none -> 12.4 us  [the longest x1 7.81 us: shards(): call(backward_body, (piece, piece), 7, [w_scratch, pltpu.VMEM((SPAN, 2 *...]
    ppermute x0 -> x2, starting transfers between devices: none -> 7.43 us  [swap(): return lax.ppermute(x, 'core', [(0, 1), (1, 0)])]
  transfers between devices with their start and end apart: 3 -> 2, of which waited for: 3 -> 1; matrix products, arithmetic and copies ran while one was open for 1% -> 0% of each run, Pallas kernels for 0% -> 2%
where the time goes in v1:
time: 136 us; the launch traced here: 134 us
  blocking collectives  109 us (80%)
  Pallas kernels  12.4 us (9%)
  starting transfers between devices  7.43 us (5%)
  waiting for transfers between devices  3.1 us (2%)
  local copies, waits for them, and re-layouts  2 us (1%)
    all_to_all x5, blocking collectives, exchange(): return lax.all_to_all(x, axes, 0, 0, tiled=True)  109 us
    pallas_call x1, Pallas kernels, shards(): call(backward_body, (piece, piece), 7, [w_scratch, pltpu.VMEM((SPAN, 2 *...  7.81 us
    ppermute x2, starting transfers between devices, swap(): return lax.ppermute(x, 'core', [(0, 1), (1, 0)])  7.43 us
    ppermute x2, waiting for transfers between devices, swap(): return lax.ppermute(x, 'core', [(0, 1), (1, 0)])  3.1 us
    pallas_call x1, Pallas kernels, shards(): call(prepare_body, (shape(TOK, GROUP * HD), shape(TOK, GROUP * HD), shape...  2.74 us
  transfers between devices with their start and end apart: 2, of which 1 were waited for; matrix products, arithmetic and copies ran while one was open for 0% of the time, Pallas kernels for 2%

profile of v1, /device:TPU:1, one launch (start us, length us, event | category | flops | bytes accessed | tf_op | source)
XLA Modules:
  0.0 134.4 jit_solution(2202684401668278802)
XLA Ops:
  0.6 0.7 dynamic_slice.3
  1.4 32.0 %all_to_all.25 = bf16[12,56,128]{2,1,0:T(8,128)(2,1)S(1)} all-to-all(bf16[12,56,128]{2,1,0:T(8,128)(2,1)S(1)} %broadcast_in_dim.9), channel_id=1, replica_groups=mesh['zh'=2,'zl'=2,'xh'=2,'xl'=2,'yh'=4,'yl'=2,'zhi'=3,'core'=2] {'yh','..., dimensions={0} | all-to-all | bytes 344064 | tf_op jit(solution)/shard_map/all_to_all | solution.py:179
  33.3 0.0 copy-start.1
  33.3 0.2 broadcast_in_dim.20
  33.5 0.0 copy-start
  33.5 0.0 copy-start.3
  33.6 0.0 copy-start.4
  33.6 0.0 copy-start.6
  33.6 20.2 %all_to_all.26.own = bf16[8,12,56,128]{3,2,1,0:T(8,128)(2,1)} all-to-all(bf16[8,12,56,128]{3,2,1,0:T(8,128)(2,1)S(1)} %broadcast_in_dim.20), channel_id=1, replica_groups=mesh['zh'=2,'zl'=2,'xh'=2,'xl'=2,'yh'=4,'yl'=2,'zhi'=3,'core'=2] {'zl','..., dimensions={0} | all-to-all | bytes 2752512 | tf_op jit(solution)/shard_map/all_to_all | solution.py:179
  53.8 5.5 %collective-permute-start = (bf16[8,12,56,128]{3,2,1,0:T(8,128)(2,1)}, bf16[8,12,56,128]{3,2,1,0:T(8,128)(2,1)}, u32[]{:S(2)}, u32[]{:S(2)}) collective-permute-start(bf16[8,12,56,128]{3,2,1,0:T(8,128)(2,1)} %all_to_all.26.own), channel_id=1, source_target_pairs={{0,1},{1,0},{2,3},{3,2},{4,5},{5,4},{6,7},{7,6},{8,9},{9,8},{10,11... | collective-permute-start | bytes 4128776 | tf_op jit(solution)/shard_map/ppermute | solution.py:183
  59.3 0.1 pad_add_fusion.where_ref
  59.4 0.0 copy-done.1
  59.4 0.0 copy-done
  59.4 0.0 copy-done.3
  59.4 0.0 copy-done.4
  59.4 0.0 copy-done.6
  59.4 0.0 copy-start.2
  59.5 1.0 copy-done.2
  60.5 0.0 copy-start.5
  60.5 0.0 copy-start.7
  60.5 2.7 %prepare.1 = (bf16[256,1024]{1,0:T(8,128)(2,1)S(1)}, bf16[256,1024]{1,0:T(8,128)(2,1)S(1)}, f32[256,256]{1,0:T(8,128)S(1)}) custom-call(s32[2]{0:T(128)S(1)} %pad_add_fusion.where_ref, bf16[256,5120]{1,0:T(8,128)(2,1)S(1)} %bitcast.8, bf16[256,1024]{1,0:T(8,128)(2,1)S(1)} %bitcast.10, bf16[256,1024]{1,0:T(8,128)(2,1)S(1)} %bitcast.11, ...), custom_call_target="tpu_custom_call" | custom-call | tf_op jit(solution)/shard_map/prepare/pallas_call | solution.py:193
  63.2 0.0 collective-permute-done.other
  63.2 0.0 copy-done.5
  63.3 0.0 copy-done.7
  63.3 7.8 %backward.1 = (bf16[8,12,56,128]{3,2,1,0:T(8,128)(2,1)S(1)}, bf16[8,12,56,128]{3,2,1,0:T(8,128)(2,1)S(1)}) custom-call(s32[2]{0:T(128)S(1)} %pad_add_fusion.where_ref, bf16[256,5120]{1,0:T(8,128)(2,1)S(1)} %bitcast.9, bf16[256,1024]{1,0:T(8,128)(2,1)S(1)} %get-tuple-element.9.q_norms, bf16[256,1024]{1,0:T(8,128)(2,1)S(1)} %get-tuple-element.10.cots, ...), custom_call_target="tpu_custom_call" | custom-call | tf_op jit(solution)/shard_map/backward/pallas_call | solution.py:197
  71.1 1.9 %collective-permute-start.1 = (bf16[8,12,56,128]{3,2,1,0:T(8,128)(2,1)S(1)}, bf16[8,12,56,128]{3,2,1,0:T(8,128)(2,1)S(1)}, u32[]{:S(2)}, u32[]{:S(2)}) collective-permute-start(bf16[8,12,56,128]{3,2,1,0:T(8,128)(2,1)S(1)} %get-tuple-element.13), channel_id=1, source_target_pairs={{0,1},{1,0},{2,3},{3,2},{4,5},{5,4},{6,7},{7,6},{8,9},{9,8},{10,11... | collective-permute-start | bytes 4128776 | tf_op jit(solution)/shard_map/ppermute | solution.py:183
  73.0 3.1 %collective-permute-done.1.received = bf16[8,12,56,128]{3,2,1,0:T(8,128)(2,1)S(1)} collective-permute-done((bf16[8,12,56,128]{3,2,1,0:T(8,128)(2,1)S(1)}, bf16[8,12,56,128]{3,2,1,0:T(8,128)(2,1)S(1)}, u32[]{:S(2)}, u32[]{:S(2)}) %collective-permute-start.1) | collective-permute-done | bytes 1376288 | tf_op jit(solution)/shard_map/ppermute | solution.py:183
  76.1 0.4 near.1
  76.5 21.1 %all_to_all.27.received = bf16[8,680,128]{2,1,0:T(8,128)(2,1)S(1)} all-to-all(bf16[8,680,128]{2,1,0:T(8,128)(2,1)S(1)} %near.1), channel_id=1, replica_groups=mesh['zh'=2,'zl'=2,'xh'=2,'xl'=2,'yh'=4,'yl'=2,'zhi'=3,'core'=2] {'zl','..., dimensions={0} | all-to-all | bytes 2785280 | tf_op jit(solution)/shard_map/all_to_all | solution.py:179
  97.6 0.7 far.1
  98.3 17.3 %all_to_all.28.received = bf16[12,64,128]{2,1,0:T(8,128)(2,1)S(1)} all-to-all(bf16[12,64,128]{2,1,0:T(8,128)(2,1)S(1)} %far.1), channel_id=1, replica_groups=mesh['zh'=2,'zl'=2,'xh'=2,'xl'=2,'yh'=4,'yl'=2,'zhi'=3,'core'=2] {'yh','..., dimensions={0} | all-to-all | bytes 393216 | tf_op jit(solution)/shard_map/all_to_all | solution.py:179
  115.7 18.1 %all_to_all.29.spread = bf16[16,64,128]{2,1,0:T(8,128)(2,1)S(1)} all-to-all(bf16[16,64,128]{2,1,0:T(8,128)(2,1)S(1)} %last.1), channel_id=1, replica_groups=mesh['zh'=2,'zl'=2,'xh'=2,'xl'=2,'yh'=4,'yl'=2,'zhi'=3,'core'=2] {'zh','..., dimensions={0} | all-to-all | bytes 524288 | tf_op jit(solution)/shard_map/all_to_all | solution.py:179
  133.7 0.7 finish.1
  (2 shorter events, 0.1 us)
Async XLA Ops:
  33.3 26.1 %copy-start.1 = (bf16[1,256,1024]{2,1,0:T(8,128)(2,1)S(1)}, bf16[1,256,1024]{2,1,0:T(8,128)(2,1)}, u32[]{:S(2)}) copy-start(bf16[1,256,1024]{2,1,0:T(8,128)(2,1)} %param.10) | copy-start | bytes 1572868
  33.5 25.9 %copy-start = (bf16[1,256,5120]{2,1,0:T(8,128)(2,1)S(1)}, bf16[1,256,5120]{2,1,0:T(8,128)(2,1)}, u32[]{:S(2)}) copy-start(bf16[1,256,5120]{2,1,0:T(8,128)(2,1)} %param.9) | copy-start | bytes 7864324
  33.5 25.9 %copy-start.3 = (f32[1,256]{1,0:T(1,128)S(1)}, f32[1,256]{1,0:T(1,128)}, u32[]{:S(2)}) copy-start(f32[1,256]{1,0:T(1,128)} %advantage.1) | copy-start | bytes 3076
  33.6 25.9 %copy-start.4 = (s32[1,256]{1,0:T(1,128)S(1)}, s32[1,256]{1,0:T(1,128)}, u32[]{:S(2)}) copy-start(s32[1,256]{1,0:T(1,128)} %selected.1) | copy-start | bytes 3076
  33.6 25.9 %copy-start.6 = (f32[128]{0:T(128)S(1)}, f32[128]{0:T(128)}, u32[]{:S(2)}) copy-start(f32[128]{0:T(128)} %param.17) | copy-start | bytes 1540
  53.8 9.4 %collective-permute-start = (bf16[8,12,56,128]{3,2,1,0:T(8,128)(2,1)}, bf16[8,12,56,128]{3,2,1,0:T(8,128)(2,1)}, u32[]{:S(2)}, u32[]{:S(2)}) collective-permute-start(bf16[8,12,56,128]{3,2,1,0:T(8,128)(2,1)} %all_to_all.26.own), channel_id=1, source_target_pairs={{0,1},{1,0},{2,3},{3,2},{4,5},{5,4},{6,7},{7,6},{8,9},{9,8},{10,11... | collective-permute-start | bytes 4128776 | tf_op jit(solution)/shard_map/ppermute | solution.py:183
  59.4 1.0 copy-start.2
  60.5 2.8 %copy-start.5 = (s32[1,256]{1,0:T(1,128)S(1)}, s32[1,256]{1,0:T(1,128)}, u32[]{:S(2)}) copy-start(s32[1,256]{1,0:T(1,128)} %segment.1) | copy-start | bytes 3076
  60.5 2.8 %copy-start.7 = (f32[128]{0:T(128)S(1)}, f32[128]{0:T(128)}, u32[]{:S(2)}) copy-start(f32[128]{0:T(128)} %param.16) | copy-start | bytes 1540
  71.1 5.0 %collective-permute-start.1 = (bf16[8,12,56,128]{3,2,1,0:T(8,128)(2,1)S(1)}, bf16[8,12,56,128]{3,2,1,0:T(8,128)(2,1)S(1)}, u32[]{:S(2)}, u32[]{:S(2)}) collective-permute-start(bf16[8,12,56,128]{3,2,1,0:T(8,128)(2,1)S(1)} %get-tuple-element.13), channel_id=1, source_target_pairs={{0,1},{1,0},{2,3},{3,2},{4,5},{5,4},{6,7},{7,6},{8,9},{9,8},{10,11... | collective-permute-start | bytes 4128776 | tf_op jit(solution)/shard_map/ppermute | solution.py:183

commit v2 on v1

--- a/solution.py
+++ b/solution.py
@@ -1,5 +1,6 @@
 import jax
 import jax.numpy as jnp
+import numpy as np
 from jax import lax
 from jax.experimental import pallas as pl
 from jax.experimental.pallas import tpu as pltpu
@@ -17,12 +18,10 @@
 BODY = FAR * HALF
 SPAN = 48 * OWN
 AXES = ("zh", "zl", "xh", "xl", "yh", "yl", "zhi", "core")
-PAIRS = ("zl", "xl", "yl")
 
 f32 = jnp.float32
 bf16 = jnp.bfloat16
 vmem = pl.BlockSpec(memory_space=pltpu.VMEM)
-smem = pl.BlockSpec(memory_space=pltpu.SMEM)
 
 
 def dot(a, b, ca, cb):
@@ -52,9 +51,13 @@
     lax.fori_loop(0, FAR, step, 0)
 
 
-def prepare_body(where_ref, hidden, queries, upstream, advantage, selected, q_gain, own, q_out, cot_out, kv_out, w):
-    place(w, own, where_ref[0])
-    kv_out[...] = dot(hidden[...], w[:D, :], 1, 0)
+def project(hidden, w):
+    return jnp.concatenate([dot(hidden[i : i + TOK // 2], w[:D, :], 1, 0) for i in (0, TOK // 2)], axis=0)
+
+
+def prepare_body(hidden, queries, upstream, advantage, selected, q_gain, own, q_out, cot_out, kv_out, w):
+    place(w, own, lax.axis_index("core"))
+    kv_out[...] = project(hidden, w)
     weight = column(advantage[...] * selected[...].astype(f32))
     for h in range(GROUP):
         cols = slice(h * HD, (h + 1) * HD)
@@ -64,10 +67,10 @@
         cot_out[:, cols] = (weight * upstream[:, cols].astype(f32)).astype(bf16)
 
 
-def backward_body(where_ref, hidden, q_norms, cots, kv_part, segment, k_gain, other, keep, send, w, acc):
-    core = where_ref[0]
+def backward_body(hidden, q_norms, cots, kv_part, segment, k_gain, other, keep, send, w, acc):
+    core = lax.axis_index("core")
     place(w, other, 1 - core)
-    kv = kv_part[...] + dot(hidden[...], w[:D, :], 1, 0)
+    kv = kv_part[...] + project(hidden, w)
     k_raw = kv[:, :HD]
     k_scale = lax.rsqrt(jnp.mean(k_raw * k_raw, axis=-1, keepdims=True) + EPS)
     k_hat = k_raw * k_scale
@@ -81,20 +84,38 @@
         [(seg_col == seg[:, i * HD : (i + 1) * HD]) & (s_col <= t_row + i * HD) for i in range(2)], axis=1
     )
     scale = HD ** (-0.5)
-    d_key = jnp.zeros((TOK, HD), f32)
-    d_value = jnp.zeros((TOK, HD), f32)
+    exponent = scale * 1.4426950408889634
+    mask_low = allowed[:HD]
+    mask_high = allowed[HD:, HD:]
+    d_key_low = d_key_high = d_value_low = d_value_high = jnp.zeros((HD, HD), f32)
     for h in range(GROUP):
         cols = slice(h * HD, (h + 1) * HD)
         q_norm = q_norms[:, cols]
         cot = cots[:, cols]
-        expo = jnp.where(allowed, jnp.exp(dot(k_norm, q_norm, 1, 1) * scale), 0.0)
-        probs = expo * (1.0 / jnp.sum(expo, axis=0, keepdims=True))
-        probs_b = probs.astype(bf16)
-        dprob = dot(values, cot, 1, 1)
-        delta = jnp.sum(probs_b.astype(f32) * dprob, axis=0, keepdims=True)
-        dscore = (probs * (dprob - delta) * scale).astype(bf16)
-        d_key = d_key + dot(dscore, q_norm, 1, 0)
-        d_value = d_value + dot(probs_b, cot, 1, 0)
+        low, high = slice(0, HD), slice(HD, TOK)
+        s_low = dot(k_norm[low], q_norm, 1, 1)
+        s_high = dot(k_norm[high], q_norm[high], 1, 1)
+        p_low = dot(values[low], cot, 1, 1)
+        p_high = dot(values[high], cot[high], 1, 1)
+        e_low = jnp.where(mask_low, jnp.exp2(s_low * exponent), 0.0)
+        e_high = jnp.where(mask_high, jnp.exp2(s_high * exponent), 0.0)
+        total = jnp.sum(e_low, axis=0, keepdims=True)
+        total = jnp.concatenate([total[:, low], total[:, high] + jnp.sum(e_high, axis=0, keepdims=True)], axis=1)
+        inverse = 1.0 / total
+        e_low = e_low * inverse
+        e_high = e_high * inverse[:, high]
+        b_low = e_low.astype(bf16)
+        b_high = e_high.astype(bf16)
+        delta = jnp.sum(b_low.astype(f32) * p_low, axis=0, keepdims=True)
+        delta = jnp.concatenate([delta[:, low], delta[:, high] + jnp.sum(b_high.astype(f32) * p_high, axis=0, keepdims=True)], axis=1)
+        g_low = (e_low * (p_low - delta) * scale).astype(bf16)
+        g_high = (e_high * (p_high - delta[:, high]) * scale).astype(bf16)
+        d_key_low = d_key_low + dot(g_low, q_norm, 1, 0)
+        d_key_high = d_key_high + dot(g_high, q_norm[high], 1, 0)
+        d_value_low = d_value_low + dot(b_low, cot, 1, 0)
+        d_value_high = d_value_high + dot(b_high, cot[high], 1, 0)
+    d_key = jnp.concatenate([d_key_low, d_key_high], axis=0)
+    d_value = jnp.concatenate([d_value_low, d_value_high], axis=0)
     gain = jnp.sum(d_key * k_hat, axis=0, keepdims=True)
     d_khat = d_key * k_gain[...]
     d_kraw = k_scale * (d_khat - k_hat * jnp.mean(d_khat * k_hat, axis=-1, keepdims=True))
@@ -132,16 +153,17 @@
     tail = gain_rows(keep[1, FAR - 1, 0:8].astype(f32) + received[1, FAR - 1, 0:8].astype(f32))
     for i in range(NEAR):
         total = (keep[i].astype(f32) + received[i].astype(f32)).reshape(BODY, HD)
+        if i % 2 == 1:
+            total = jnp.concatenate([total[: BODY - HALF], jnp.zeros((HALF, HD), f32)], axis=0)
         blocks[i] = jnp.concatenate([total, tail], axis=0).astype(bf16)
 
 
-def far_body(where_ref, received, blocks):
-    tail = gain_rows(sum(received[i, BODY : BODY + 8].astype(f32) for i in range(NEAR)))
-    for far in range(FAR):
-        total = sum(received[i, far * HALF : (far + 1) * HALF].astype(f32) for i in range(NEAR))
-        if far == FAR - 1:
-            total = jnp.where(where_ref[1] == 1, 0.0, total)
-        blocks[far] = jnp.concatenate([total, tail], axis=0).astype(bf16)
+def far_body(received, blocks):
+    tail = gain_rows(sum(received[i, BODY:].astype(f32) for i in range(NEAR)))
+    for far in range(0, FAR, 2):
+        total = sum(received[i, far * HALF : (far + 2) * HALF].astype(f32) for i in range(NEAR))
+        for i in range(2):
+            blocks[far + i] = jnp.concatenate([total[i * HALF : (i + 1) * HALF], tail], axis=0).astype(bf16)
 
 
 def last_body(received, blocks):
@@ -159,11 +181,11 @@
     d_gain[...] = total[0][HALF : HALF + 1] + total[0][HALF + 1 : HALF + 2]
 
 
-def call(body, out, n_vector, scratch, limit, name, scalars=0):
+def call(body, out, n_vector, scratch, limit, name):
     return pl.pallas_call(
         body,
         out_shape=out,
-        in_specs=[smem] * scalars + [vmem] * n_vector,
+        in_specs=[vmem] * n_vector,
         out_specs=jax.tree.map(lambda _: vmem, out),
         scratch_shapes=scratch,
         compiler_params=pltpu.CompilerParams(vmem_limit_bytes=limit << 20),
@@ -175,8 +197,23 @@
     return jax.ShapeDtypeStruct(dims, dtype)
 
 
-def exchange(x, axes):
-    return lax.all_to_all(x, axes, 0, 0, tiled=True)
+def near_groups():
+    ids = np.arange(16 * 48).reshape(4, 4, 8, 3, 2)
+    groups = []
+    for core in range(2):
+        for z in range(core, 12, 2):
+            for x in range(core, 4, 2):
+                for y in range(core, 8, 2):
+                    members = [0] * NEAR
+                    for i in range(NEAR):
+                        mz, mx, my = (z + i // 4) % 12, (x + i // 2 % 2) % 4, (y + i % 2) % 8
+                        members[4 * (mz % 2) + 2 * (mx % 2) + my % 2] = int(ids[mz % 4, mx, my, mz // 4, core])
+                    groups.append(members)
+    return groups
+
+
+def exchange(x, axes, groups=None):
+    return lax.all_to_all(x, axes, 0, 0, tiled=True, axis_index_groups=groups)
 
 
 def swap(x):
@@ -184,21 +221,20 @@
 
 
 def shards(hidden, queries, upstream, advantage, selected, segment, w_kv, k_gain, q_gain):
-    where = jnp.stack([lax.axis_index("core"), lax.axis_index("yl")]).astype(jnp.int32)
     mine = lax.dynamic_slice(w_kv, (lax.axis_index("xl") * HALF, lax.axis_index("zl") * HD), (HALF, HD))
     part = exchange(jnp.broadcast_to(mine[None], (FAR, HALF, HD)), ("yh", "zhi"))
-    own = exchange(jnp.broadcast_to(part[None], (NEAR, FAR, HALF, HD)), PAIRS)
+    own = exchange(jnp.broadcast_to(part[None], (NEAR, FAR, HALF, HD)), AXES, near_groups())
     other = swap(own)
     w_scratch = pltpu.VMEM((SPAN, 2 * HD), bf16)
     q_norms, cots, kv_part = call(
-        prepare_body, (shape(TOK, GROUP * HD), shape(TOK, GROUP * HD), shape(TOK, 2 * HD, dtype=f32)), 7, [w_scratch], 16, "prepare", 1
-    )(where, hidden[0], queries[0], upstream[0], advantage, selected, q_gain[None], own)
+        prepare_body, (shape(TOK, GROUP * HD), shape(TOK, GROUP * HD), shape(TOK, 2 * HD, dtype=f32)), 7, [w_scratch], 16, "prepare"
+    )(hidden[0], queries[0], upstream[0], advantage, selected, q_gain[None], own)
     piece = shape(NEAR, FAR, HALF, HD)
-    keep, send = call(backward_body, (piece, piece), 7, [w_scratch, pltpu.VMEM((SPAN, 2 * HD), f32)], 24, "backward", 1)(
-        where, hidden[0], q_norms, cots, kv_part, segment, k_gain[None], other
+    keep, send = call(backward_body, (piece, piece), 7, [w_scratch, pltpu.VMEM((SPAN, 2 * HD), f32)], 24, "backward")(
+        hidden[0], q_norms, cots, kv_part, segment, k_gain[None], other
     )
     blocks = call(near_body, shape(NEAR, BODY + 8, HD), 2, [], 12, "near")(keep, swap(send))
-    blocks = call(far_body, shape(FAR, HALF + 8, HD), 1, [], 12, "far", 1)(where, exchange(blocks, PAIRS))
+    blocks = call(far_body, shape(FAR, HALF + 8, HD), 1, [], 12, "far")(exchange(blocks, AXES, near_groups()))
     blocks = call(last_body, shape(16, HALF + 8, HD), 1, [], 8, "last")(exchange(blocks, ("yh", "zhi")))
     spread = exchange(blocks, ("zh", "zl", "xh", "xl"))
     d_weight, d_gain = call(finish_body, (shape(OWN, 2 * HD, dtype=f32), shape(1, HD, dtype=f32)), 1, [], 4, "finish")(spread)

time: 136 us -> 127 us (0.934)
  Pallas kernels: 12.4 us -> 7.95 us
  starting transfers between devices: 7.43 us -> 3.94 us
  waiting for transfers between devices: 3.1 us -> 4.51 us
    ppermute x2, starting transfers between devices: 7.43 us -> 3.94 us  [swap(): return lax.ppermute(x, 'core', [(0, 1), (1, 0)])]
    pallas_call x1, Pallas kernels: 7.81 us -> 5.27 us  [shards(): call(backward_body, (piece, piece), 7, [w_scratch, pltpu.VMEM((SPAN, 2 *...]
    ppermute x2, waiting for transfers between devices: 3.1 us -> 4.51 us  [swap(): return lax.ppermute(x, 'core', [(0, 1), (1, 0)])]
  transfers between devices with their start and end apart: 2 -> 2, of which waited for: 1 -> 2; matrix products, arithmetic and copies ran while one was open for 0% -> 0% of each run, Pallas kernels for 2% -> 1%
where the time goes in v2:
time: 127 us
  blocking collectives  108 us (85%)
  Pallas kernels  7.95 us (6%)
  waiting for transfers between devices  4.51 us (4%)
  starting transfers between devices  3.94 us (3%)
    all_to_all x5, blocking collectives, exchange(): return lax.all_to_all(x, axes, 0, 0, tiled=True, axis_index_groups=groups)  108 us
    pallas_call x1, Pallas kernels, shards(): call(backward_body, (piece, piece), 7, [w_scratch, pltpu.VMEM((SPAN, 2 *...  5.27 us
    ppermute x2, waiting for transfers between devices, swap(): return lax.ppermute(x, 'core', [(0, 1), (1, 0)])  4.51 us
    ppermute x2, starting transfers between devices, swap(): return lax.ppermute(x, 'core', [(0, 1), (1, 0)])  3.94 us
  transfers between devices with their start and end apart: 2, of which 2 were waited for; matrix products, arithmetic and copies ran while one was open for 0% of the time, Pallas kernels for 1%

profile of v2, /device:TPU:1, one launch (start us, length us, event | category | flops | bytes accessed | tf_op | source)
XLA Modules:
  0.0 126.6 jit_solution(16245225808665593897)
XLA Ops:
  0.6 0.7 dynamic_slice.3
  1.4 32.0 %all_to_all.25 = bf16[12,56,128]{2,1,0:T(8,128)(2,1)S(1)} all-to-all(bf16[12,56,128]{2,1,0:T(8,128)(2,1)S(1)} %broadcast_in_dim.9), channel_id=1, replica_groups=mesh['zh'=2,'zl'=2,'xh'=2,'xl'=2,'yh'=4,'yl'=2,'zhi'=3,'core'=2] {'yh','..., dimensions={0} | all-to-all | bytes 344064 | tf_op jit(solution)/shard_map/all_to_all | solution.py:216
  33.3 0.0 copy-start.1
  33.3 0.0 copy-start.2
  33.3 0.2 broadcast_in_dim.20
  33.5 0.0 copy-start
  33.5 0.0 copy-start.3
  33.6 0.0 copy-start.4
  33.6 0.0 copy-start.6
  33.6 24.8 %all_to_all.26.own = bf16[8,12,56,128]{3,2,1,0:T(8,128)(2,1)S(1)} all-to-all(bf16[8,12,56,128]{3,2,1,0:T(8,128)(2,1)S(1)} %broadcast_in_dim.20), channel_id=1, replica_groups={{0,6,48,54,192,198,240,246},{12,18,60,66,204,210,252,258},{24,30,72,78,..., dimensions={0} | all-to-all | bytes 2752512 | tf_op jit(solution)/shard_map/all_to_all | solution.py:216
  58.4 1.9 %collective-permute-start = (bf16[8,12,56,128]{3,2,1,0:T(8,128)(2,1)S(1)}, bf16[8,12,56,128]{3,2,1,0:T(8,128)(2,1)S(1)}, u32[]{:S(2)}, u32[]{:S(2)}) collective-permute-start(bf16[8,12,56,128]{3,2,1,0:T(8,128)(2,1)S(1)} %all_to_all.26.own), channel_id=1, source_target_pairs={{0,1},{1,0},{2,3},{3,2},{4,5},{5,4},{6,7},{7,6},{8,9},{9,8},{10,11... | collective-permute-start | bytes 4128776 | tf_op jit(solution)/shard_map/ppermute | solution.py:220
  60.3 0.0 copy-done.1
  60.3 0.0 copy-done.2
  60.3 0.0 copy-done
  60.3 0.0 copy-done.3
  60.3 0.0 copy-done.4
  60.3 0.0 copy-done.6
  60.3 0.0 copy-start.5
  60.3 0.0 copy-start.7
  60.4 1.5 %prepare.1 = (bf16[256,1024]{1,0:T(8,128)(2,1)S(1)}, bf16[256,1024]{1,0:T(8,128)(2,1)S(1)}, f32[256,256]{1,0:T(8,128)S(1)}) custom-call(bf16[256,5120]{1,0:T(8,128)(2,1)S(1)} %bitcast.6, bf16[256,1024]{1,0:T(8,128)(2,1)S(1)} %bitcast.8, bf16[256,1024]{1,0:T(8,128)(2,1)S(1)} %bitcast.9, f32[1,256]{1,0:T(1,128)S(1)} %copy-done.3, s32[1,256]{1,0:T(1,128)S(1)} %copy-done.4, ...), custom_call_target="tpu_custom_call" | custom-call | tf_op jit(solution)/shard_map/prepare/pallas_call | solution.py:229
  61.8 1.5 %collective-permute-done.other = bf16[8,12,56,128]{3,2,1,0:T(8,128)(2,1)S(1)} collective-permute-done((bf16[8,12,56,128]{3,2,1,0:T(8,128)(2,1)S(1)}, bf16[8,12,56,128]{3,2,1,0:T(8,128)(2,1)S(1)}, u32[]{:S(2)}, u32[]{:S(2)}) %collective-permute-start) | collective-permute-done | bytes 1376288 | tf_op jit(solution)/shard_map/ppermute | solution.py:220
  63.4 0.0 copy-done.5
  63.4 0.0 copy-done.7
  63.4 5.3 %backward.1 = (bf16[8,12,56,128]{3,2,1,0:T(8,128)(2,1)S(1)}, bf16[8,12,56,128]{3,2,1,0:T(8,128)(2,1)S(1)}) custom-call(bf16[256,5120]{1,0:T(8,128)(2,1)S(1)} %bitcast.7, bf16[256,1024]{1,0:T(8,128)(2,1)S(1)} %get-tuple-element.9.q_norms, bf16[256,1024]{1,0:T(8,128)(2,1)S(1)} %get-tuple-element.10.cots, f32[256,256]{1,0:T(8,128)S(1)} %get-tuple-element.11.kv_part, ...), custom_call_target="tpu_custom_call" | custom-call | tf_op jit(solution)/shard_map/backward/pallas_call | solution.py:233
  68.6 2.0 %collective-permute-start.1 = (bf16[8,12,56,128]{3,2,1,0:T(8,128)(2,1)S(1)}, bf16[8,12,56,128]{3,2,1,0:T(8,128)(2,1)S(1)}, u32[]{:S(2)}, u32[]{:S(2)}) collective-permute-start(bf16[8,12,56,128]{3,2,1,0:T(8,128)(2,1)S(1)} %get-tuple-element.13), channel_id=1, source_target_pairs={{0,1},{1,0},{2,3},{3,2},{4,5},{5,4},{6,7},{7,6},{8,9},{9,8},{10,11... | collective-permute-start | bytes 4128776 | tf_op jit(solution)/shard_map/ppermute | solution.py:220
  70.7 3.0 %collective-permute-done.1.received = bf16[8,12,56,128]{3,2,1,0:T(8,128)(2,1)S(1)} collective-permute-done((bf16[8,12,56,128]{3,2,1,0:T(8,128)(2,1)S(1)}, bf16[8,12,56,128]{3,2,1,0:T(8,128)(2,1)S(1)}, u32[]{:S(2)}, u32[]{:S(2)}) %collective-permute-start.1) | collective-permute-done | bytes 1376288 | tf_op jit(solution)/shard_map/ppermute | solution.py:220
  73.7 0.3 near.1
  74.0 17.8 %all_to_all.27.received = bf16[8,680,128]{2,1,0:T(8,128)(2,1)S(1)} all-to-all(bf16[8,680,128]{2,1,0:T(8,128)(2,1)S(1)} %near.1), channel_id=1, replica_groups={{0,6,48,54,192,198,240,246},{12,18,60,66,204,210,252,258},{24,30,72,78,..., dimensions={0} | all-to-all | bytes 2785280 | tf_op jit(solution)/shard_map/all_to_all | solution.py:216
  91.8 0.2 far.1
  92.0 21.2 %all_to_all.28.received = bf16[12,64,128]{2,1,0:T(8,128)(2,1)S(1)} all-to-all(bf16[12,64,128]{2,1,0:T(8,128)(2,1)S(1)} %far.1), channel_id=1, replica_groups=mesh['zh'=2,'zl'=2,'xh'=2,'xl'=2,'yh'=4,'yl'=2,'zhi'=3,'core'=2] {'yh','..., dimensions={0} | all-to-all | bytes 393216 | tf_op jit(solution)/shard_map/all_to_all | solution.py:216
  113.2 12.7 %all_to_all.29.spread = bf16[16,64,128]{2,1,0:T(8,128)(2,1)S(1)} all-to-all(bf16[16,64,128]{2,1,0:T(8,128)(2,1)S(1)} %last.1), channel_id=1, replica_groups=mesh['zh'=2,'zl'=2,'xh'=2,'xl'=2,'yh'=4,'yl'=2,'zhi'=3,'core'=2] {'zh','..., dimensions={0} | all-to-all | bytes 524288 | tf_op jit(solution)/shard_map/all_to_all | solution.py:216
  125.9 0.7 finish.1
  (2 shorter events, 0.1 us)
Async XLA Ops:
  33.3 26.9 %copy-start.1 = (bf16[1,256,1024]{2,1,0:T(8,128)(2,1)S(1)}, bf16[1,256,1024]{2,1,0:T(8,128)(2,1)}, u32[]{:S(2)}) copy-start(bf16[1,256,1024]{2,1,0:T(8,128)(2,1)} %param.10) | copy-start | bytes 1572868
  33.3 26.9 %copy-start.2 = (bf16[1,256,1024]{2,1,0:T(8,128)(2,1)S(1)}, bf16[1,256,1024]{2,1,0:T(8,128)(2,1)}, u32[]{:S(2)}) copy-start(bf16[1,256,1024]{2,1,0:T(8,128)(2,1)} %param.11) | copy-start | bytes 1572868
  33.5 26.8 %copy-start = (bf16[1,256,5120]{2,1,0:T(8,128)(2,1)S(1)}, bf16[1,256,5120]{2,1,0:T(8,128)(2,1)}, u32[]{:S(2)}) copy-start(bf16[1,256,5120]{2,1,0:T(8,128)(2,1)} %param.9) | copy-start | bytes 7864324
  33.5 26.8 %copy-start.3 = (f32[1,256]{1,0:T(1,128)S(1)}, f32[1,256]{1,0:T(1,128)}, u32[]{:S(2)}) copy-start(f32[1,256]{1,0:T(1,128)} %advantage.1) | copy-start | bytes 3076
  33.6 26.8 %copy-start.4 = (s32[1,256]{1,0:T(1,128)S(1)}, s32[1,256]{1,0:T(1,128)}, u32[]{:S(2)}) copy-start(s32[1,256]{1,0:T(1,128)} %selected.1) | copy-start | bytes 3076
  33.6 26.8 %copy-start.6 = (f32[128]{0:T(128)S(1)}, f32[128]{0:T(128)}, u32[]{:S(2)}) copy-start(f32[128]{0:T(128)} %param.17) | copy-start | bytes 1540
  58.4 5.0 %collective-permute-start = (bf16[8,12,56,128]{3,2,1,0:T(8,128)(2,1)S(1)}, bf16[8,12,56,128]{3,2,1,0:T(8,128)(2,1)S(1)}, u32[]{:S(2)}, u32[]{:S(2)}) collective-permute-start(bf16[8,12,56,128]{3,2,1,0:T(8,128)(2,1)S(1)} %all_to_all.26.own), channel_id=1, source_target_pairs={{0,1},{1,0},{2,3},{3,2},{4,5},{5,4},{6,7},{7,6},{8,9},{9,8},{10,11... | collective-permute-start | bytes 4128776 | tf_op jit(solution)/shard_map/ppermute | solution.py:220
  60.3 3.0 %copy-start.5 = (s32[1,256]{1,0:T(1,128)S(1)}, s32[1,256]{1,0:T(1,128)}, u32[]{:S(2)}) copy-start(s32[1,256]{1,0:T(1,128)} %segment.1) | copy-start | bytes 3076
  60.3 3.0 %copy-start.7 = (f32[128]{0:T(128)S(1)}, f32[128]{0:T(128)}, u32[]{:S(2)}) copy-start(f32[128]{0:T(128)} %param.16) | copy-start | bytes 1540
  68.6 5.0 %collective-permute-start.1 = (bf16[8,12,56,128]{3,2,1,0:T(8,128)(2,1)S(1)}, bf16[8,12,56,128]{3,2,1,0:T(8,128)(2,1)S(1)}, u32[]{:S(2)}, u32[]{:S(2)}) collective-permute-start(bf16[8,12,56,128]{3,2,1,0:T(8,128)(2,1)S(1)} %get-tuple-element.13), channel_id=1, source_target_pairs={{0,1},{1,0},{2,3},{3,2},{4,5},{5,4},{6,7},{7,6},{8,9},{9,8},{10,11... | collective-permute-start | bytes 4128776 | tf_op jit(solution)/shard_map/ppermute | solution.py:220

commit v3 on v2

--- a/solution.py
+++ b/solution.py
@@ -163,18 +163,20 @@
     for far in range(0, FAR, 2):
         total = sum(received[i, far * HALF : (far + 2) * HALF].astype(f32) for i in range(NEAR))
         for i in range(2):
-            blocks[far + i] = jnp.concatenate([total[i * HALF : (i + 1) * HALF], tail], axis=0).astype(bf16)
+            block = jnp.concatenate([total[i * HALF : (i + 1) * HALF], tail], axis=0).astype(bf16)
+            blocks[far + i] = block
+            blocks[FAR + far + i] = block
 
 
 def last_body(received, blocks):
-    total = sum(received[i].astype(f32) for i in range(FAR))
+    total = sum(received[i].astype(f32) for i in range(2 * FAR))
     whole = jnp.concatenate([total[:HALF], gain_rows(total[HALF:])], axis=0).astype(bf16)
-    for i in range(16):
+    for i in range(8):
         blocks[i] = whole
 
 
 def finish_body(spread, d_weight, d_gain):
-    total = [sum(spread[8 * (i // 2) + 4 * (q // 2) + 2 * (i % 2) + q % 2].astype(f32) for i in range(4)) for q in range(4)]
+    total = [sum(spread[4 * i + q].astype(f32) for i in range(2)) for q in range(4)]
     for q in range(4):
         row, col = (q % 2) * HALF, (q // 2) * HD
         d_weight[row : row + HALF, col : col + HD] = total[q][:HALF]
@@ -234,9 +236,9 @@
         hidden[0], q_norms, cots, kv_part, segment, k_gain[None], other
     )
     blocks = call(near_body, shape(NEAR, BODY + 8, HD), 2, [], 12, "near")(keep, swap(send))
-    blocks = call(far_body, shape(FAR, HALF + 8, HD), 1, [], 12, "far")(exchange(blocks, AXES, near_groups()))
-    blocks = call(last_body, shape(16, HALF + 8, HD), 1, [], 8, "last")(exchange(blocks, ("yh", "zhi")))
-    spread = exchange(blocks, ("zh", "zl", "xh", "xl"))
+    blocks = call(far_body, shape(2 * FAR, HALF + 8, HD), 1, [], 12, "far")(exchange(blocks, AXES, near_groups()))
+    blocks = call(last_body, shape(8, HALF + 8, HD), 1, [], 8, "last")(exchange(blocks, ("xh", "yh", "zhi")))
+    spread = exchange(blocks, ("zh", "zl", "xl"))
     d_weight, d_gain = call(finish_body, (shape(OWN, 2 * HD, dtype=f32), shape(1, HD, dtype=f32)), 1, [], 4, "finish")(spread)
     return (d_weight, d_gain[0])
 

time: 127 us -> 131 us (1.031)
  blocking collectives: 108 us -> 112 us
    all_to_all x5, blocking collectives: 108 us -> 112 us  [exchange(): return lax.all_to_all(x, axes, 0, 0, tiled=True, axis_index_groups=groups)]
where the time goes in v3:
time: 131 us; the launch traced here: 130 us
  blocking collectives  112 us (85%)
  Pallas kernels  7.96 us (6%)
  waiting for transfers between devices  4.51 us (3%)
  starting transfers between devices  3.94 us (3%)
    all_to_all x5, blocking collectives, exchange(): return lax.all_to_all(x, axes, 0, 0, tiled=True, axis_index_groups=groups)  112 us
    pallas_call x1, Pallas kernels, shards(): call(backward_body, (piece, piece), 7, [w_scratch, pltpu.VMEM((SPAN, 2 *...  5.27 us
    ppermute x2, waiting for transfers between devices, swap(): return lax.ppermute(x, 'core', [(0, 1), (1, 0)])  4.51 us
    ppermute x2, starting transfers between devices, swap(): return lax.ppermute(x, 'core', [(0, 1), (1, 0)])  3.94 us
  transfers between devices with their start and end apart: 2, of which 2 were waited for; matrix products, arithmetic and copies ran while one was open for 0% of the time, Pallas kernels for 1%

profile of v3, /device:TPU:1, one launch (start us, length us, event | category | flops | bytes accessed | tf_op | source)
XLA Modules:
  0.0 130.2 jit_solution(323990793441915388)
XLA Ops:
  0.6 0.7 dynamic_slice.3
  1.4 32.0 %all_to_all.25 = bf16[12,56,128]{2,1,0:T(8,128)(2,1)S(1)} all-to-all(bf16[12,56,128]{2,1,0:T(8,128)(2,1)S(1)} %broadcast_in_dim.9), channel_id=1, replica_groups=mesh['zh'=2,'zl'=2,'xh'=2,'xl'=2,'yh'=4,'yl'=2,'zhi'=3,'core'=2] {'yh','..., dimensions={0} | all-to-all | bytes 344064 | tf_op jit(solution)/shard_map/all_to_all | solution.py:218
  33.3 0.0 copy-start.1
  33.3 0.0 copy-start.2
  33.3 0.2 broadcast_in_dim.20
  33.5 0.0 copy-start
  33.5 0.0 copy-start.3
  33.6 0.0 copy-start.4
  33.6 0.0 copy-start.6
  33.6 24.8 %all_to_all.26.own = bf16[8,12,56,128]{3,2,1,0:T(8,128)(2,1)S(1)} all-to-all(bf16[8,12,56,128]{3,2,1,0:T(8,128)(2,1)S(1)} %broadcast_in_dim.20), channel_id=1, replica_groups={{0,6,48,54,192,198,240,246},{12,18,60,66,204,210,252,258},{24,30,72,78,..., dimensions={0} | all-to-all | bytes 2752512 | tf_op jit(solution)/shard_map/all_to_all | solution.py:218
  58.4 1.9 %collective-permute-start = (bf16[8,12,56,128]{3,2,1,0:T(8,128)(2,1)S(1)}, bf16[8,12,56,128]{3,2,1,0:T(8,128)(2,1)S(1)}, u32[]{:S(2)}, u32[]{:S(2)}) collective-permute-start(bf16[8,12,56,128]{3,2,1,0:T(8,128)(2,1)S(1)} %all_to_all.26.own), channel_id=1, source_target_pairs={{0,1},{1,0},{2,3},{3,2},{4,5},{5,4},{6,7},{7,6},{8,9},{9,8},{10,11... | collective-permute-start | bytes 4128776 | tf_op jit(solution)/shard_map/ppermute | solution.py:222
  60.3 0.0 copy-done.1
  60.3 0.0 copy-done.2
  60.3 0.0 copy-done
  60.3 0.0 copy-done.3
  60.3 0.0 copy-done.4
  60.3 0.0 copy-done.6
  60.3 0.0 copy-start.5
  60.3 0.0 copy-start.7
  60.4 1.5 %prepare.1 = (bf16[256,1024]{1,0:T(8,128)(2,1)S(1)}, bf16[256,1024]{1,0:T(8,128)(2,1)S(1)}, f32[256,256]{1,0:T(8,128)S(1)}) custom-call(bf16[256,5120]{1,0:T(8,128)(2,1)S(1)} %bitcast.6, bf16[256,1024]{1,0:T(8,128)(2,1)S(1)} %bitcast.8, bf16[256,1024]{1,0:T(8,128)(2,1)S(1)} %bitcast.9, f32[1,256]{1,0:T(1,128)S(1)} %copy-done.3, s32[1,256]{1,0:T(1,128)S(1)} %copy-done.4, ...), custom_call_target="tpu_custom_call" | custom-call | tf_op jit(solution)/shard_map/prepare/pallas_call | solution.py:231
  61.8 1.5 %collective-permute-done.other = bf16[8,12,56,128]{3,2,1,0:T(8,128)(2,1)S(1)} collective-permute-done((bf16[8,12,56,128]{3,2,1,0:T(8,128)(2,1)S(1)}, bf16[8,12,56,128]{3,2,1,0:T(8,128)(2,1)S(1)}, u32[]{:S(2)}, u32[]{:S(2)}) %collective-permute-start) | collective-permute-done | bytes 1376288 | tf_op jit(solution)/shard_map/ppermute | solution.py:222
  63.4 0.0 copy-done.5
  63.4 0.0 copy-done.7
  63.4 5.3 %backward.1 = (bf16[8,12,56,128]{3,2,1,0:T(8,128)(2,1)S(1)}, bf16[8,12,56,128]{3,2,1,0:T(8,128)(2,1)S(1)}) custom-call(bf16[256,5120]{1,0:T(8,128)(2,1)S(1)} %bitcast.7, bf16[256,1024]{1,0:T(8,128)(2,1)S(1)} %get-tuple-element.9.q_norms, bf16[256,1024]{1,0:T(8,128)(2,1)S(1)} %get-tuple-element.10.cots, f32[256,256]{1,0:T(8,128)S(1)} %get-tuple-element.11.kv_part, ...), custom_call_target="tpu_custom_call" | custom-call | tf_op jit(solution)/shard_map/backward/pallas_call | solution.py:235
  68.6 2.0 %collective-permute-start.1 = (bf16[8,12,56,128]{3,2,1,0:T(8,128)(2,1)S(1)}, bf16[8,12,56,128]{3,2,1,0:T(8,128)(2,1)S(1)}, u32[]{:S(2)}, u32[]{:S(2)}) collective-permute-start(bf16[8,12,56,128]{3,2,1,0:T(8,128)(2,1)S(1)} %get-tuple-element.13), channel_id=1, source_target_pairs={{0,1},{1,0},{2,3},{3,2},{4,5},{5,4},{6,7},{7,6},{8,9},{9,8},{10,11... | collective-permute-start | bytes 4128776 | tf_op jit(solution)/shard_map/ppermute | solution.py:222
  70.7 3.0 %collective-permute-done.1.received = bf16[8,12,56,128]{3,2,1,0:T(8,128)(2,1)S(1)} collective-permute-done((bf16[8,12,56,128]{3,2,1,0:T(8,128)(2,1)S(1)}, bf16[8,12,56,128]{3,2,1,0:T(8,128)(2,1)S(1)}, u32[]{:S(2)}, u32[]{:S(2)}) %collective-permute-start.1) | collective-permute-done | bytes 1376288 | tf_op jit(solution)/shard_map/ppermute | solution.py:222
  73.7 0.3 near.1
  74.0 17.8 %all_to_all.27.received = bf16[8,680,128]{2,1,0:T(8,128)(2,1)S(1)} all-to-all(bf16[8,680,128]{2,1,0:T(8,128)(2,1)S(1)} %near.1), channel_id=1, replica_groups={{0,6,48,54,192,198,240,246},{12,18,60,66,204,210,252,258},{24,30,72,78,..., dimensions={0} | all-to-all | bytes 2785280 | tf_op jit(solution)/shard_map/all_to_all | solution.py:218
  91.8 0.2 far.1
  92.0 28.8 %all_to_all.28.received = bf16[24,64,128]{2,1,0:T(8,128)(2,1)S(1)} all-to-all(bf16[24,64,128]{2,1,0:T(8,128)(2,1)S(1)} %far.1), channel_id=1, replica_groups=mesh['zh'=2,'zl'=2,'xh'=2,'xl'=2,'yh'=4,'yl'=2,'zhi'=3,'core'=2] {'xh','..., dimensions={0} | all-to-all | bytes 786432 | tf_op jit(solution)/shard_map/all_to_all | solution.py:218
  120.8 0.1 last.1
  120.8 8.7 %all_to_all.29.spread = bf16[8,64,128]{2,1,0:T(8,128)(2,1)S(1)} all-to-all(bf16[8,64,128]{2,1,0:T(8,128)(2,1)S(1)} %last.1), channel_id=1, replica_groups=mesh['zh'=2,'zl'=2,'xh'=2,'xl'=2,'yh'=4,'yl'=2,'zhi'=3,'core'=2] {'zh','..., dimensions={0} | all-to-all | bytes 262144 | tf_op jit(solution)/shard_map/all_to_all | solution.py:218
  129.5 0.7 finish.1
  (1 shorter events, 0.0 us)
Async XLA Ops:
  33.3 26.9 %copy-start.1 = (bf16[1,256,1024]{2,1,0:T(8,128)(2,1)S(1)}, bf16[1,256,1024]{2,1,0:T(8,128)(2,1)}, u32[]{:S(2)}) copy-start(bf16[1,256,1024]{2,1,0:T(8,128)(2,1)} %param.10) | copy-start | bytes 1572868
  33.3 26.9 %copy-start.2 = (bf16[1,256,1024]{2,1,0:T(8,128)(2,1)S(1)}, bf16[1,256,1024]{2,1,0:T(8,128)(2,1)}, u32[]{:S(2)}) copy-start(bf16[1,256,1024]{2,1,0:T(8,128)(2,1)} %param.11) | copy-start | bytes 1572868
  33.5 26.8 %copy-start = (bf16[1,256,5120]{2,1,0:T(8,128)(2,1)S(1)}, bf16[1,256,5120]{2,1,0:T(8,128)(2,1)}, u32[]{:S(2)}) copy-start(bf16[1,256,5120]{2,1,0:T(8,128)(2,1)} %param.9) | copy-start | bytes 7864324
  33.5 26.8 %copy-start.3 = (f32[1,256]{1,0:T(1,128)S(1)}, f32[1,256]{1,0:T(1,128)}, u32[]{:S(2)}) copy-start(f32[1,256]{1,0:T(1,128)} %advantage.1) | copy-start | bytes 3076
  33.6 26.8 %copy-start.4 = (s32[1,256]{1,0:T(1,128)S(1)}, s32[1,256]{1,0:T(1,128)}, u32[]{:S(2)}) copy-start(s32[1,256]{1,0:T(1,128)} %selected.1) | copy-start | bytes 3076
  33.6 26.8 %copy-start.6 = (f32[128]{0:T(128)S(1)}, f32[128]{0:T(128)}, u32[]{:S(2)}) copy-start(f32[128]{0:T(128)} %param.17) | copy-start | bytes 1540
  58.4 5.0 %collective-permute-start = (bf16[8,12,56,128]{3,2,1,0:T(8,128)(2,1)S(1)}, bf16[8,12,56,128]{3,2,1,0:T(8,128)(2,1)S(1)}, u32[]{:S(2)}, u32[]{:S(2)}) collective-permute-start(bf16[8,12,56,128]{3,2,1,0:T(8,128)(2,1)S(1)} %all_to_all.26.own), channel_id=1, source_target_pairs={{0,1},{1,0},{2,3},{3,2},{4,5},{5,4},{6,7},{7,6},{8,9},{9,8},{10,11... | collective-permute-start | bytes 4128776 | tf_op jit(solution)/shard_map/ppermute | solution.py:222
  60.3 3.0 %copy-start.5 = (s32[1,256]{1,0:T(1,128)S(1)}, s32[1,256]{1,0:T(1,128)}, u32[]{:S(2)}) copy-start(s32[1,256]{1,0:T(1,128)} %segment.1) | copy-start | bytes 3076
  60.3 3.0 %copy-start.7 = (f32[128]{0:T(128)S(1)}, f32[128]{0:T(128)}, u32[]{:S(2)}) copy-start(f32[128]{0:T(128)} %param.16) | copy-start | bytes 1540
  68.6 5.0 %collective-permute-start.1 = (bf16[8,12,56,128]{3,2,1,0:T(8,128)(2,1)S(1)}, bf16[8,12,56,128]{3,2,1,0:T(8,128)(2,1)S(1)}, u32[]{:S(2)}, u32[]{:S(2)}) collective-permute-start(bf16[8,12,56,128]{3,2,1,0:T(8,128)(2,1)S(1)} %get-tuple-element.13), channel_id=1, source_target_pairs={{0,1},{1,0},{2,3},{3,2},{4,5},{5,4},{6,7},{7,6},{8,9},{9,8},{10,11... | collective-permute-start | bytes 4128776 | tf_op jit(solution)/shard_map/ppermute | solution.py:222
